TPU v7x, 512 devices: a whole 4x4x16 slice. The times are simulated.
512 devices in a mesh: group: 32 (over x, y, core), tp: 16 (over z).
Axes of the slice: x: 4, y: 4, z: 16, core: 2. Of those that a mesh axis runs over, the one named last changes fastest.
Arguments:
- tokens: bfloat16 [24576, 8192], P('group', 'tp'), may hold values from -6 to 6
- w_query: bfloat16 [8192, 4096], P(None, 'tp'), may hold values from -0.0625 to 0.0625
- adapter_down: bfloat16 [384, 16, 8192], P('group', None, 'tp'), may hold values from -0.0625 to 0.0625
- adapter_up: bfloat16 [384, 16, 4096], P('group', None, 'tp'), may hold values from -1.5 to 1.5
- adapter_id: int32 [24576], P('group'), may hold values from 0 to 383, as said below
Outputs:
- query: bfloat16 [24576, 4096], P('group', 'tp')
Inputs may be any that keep to these rules, and one draw needn't show every extreme that they name: `adapter_id`: adapter a is owned by group a // 12. Among the 768 requests of one group (an aligned block), at most 48 use adapters of any one owner; in every draw one owner receives exactly 48 from every group.
All inputs are finite; a program needn't handle non-finite values.
Results may differ from a plain program's by a relative error of at most 0.014.
Values may be sent and summed in bfloat16 or wider, within the bound.
No kernel may reach another device: no remote copies, remote signals or barrier semaphores. Data moves between devices by JAX's collectives and lax.ppermute only.
A program may use at most 128 MiB of HBM per device.

v0:
```python
import jax
import jax.numpy as jnp
from jax import lax
from jax.sharding import PartitionSpec as P

adapter_scale_factor = 2.0
owner_slots = 48
F32, BF16 = (jnp.float32, jnp.bfloat16)


def slot_of_request(adapter_id, groups, per_group):
    n = adapter_id.shape[0]
    owner = adapter_id // per_group
    to_owner = owner[:, None] == lax.broadcasted_iota(jnp.int32, (n, groups), 1)
    before = lax.broadcasted_iota(jnp.int32, (n, n), 0) > lax.broadcasted_iota(jnp.int32, (n, n), 1)
    count = jnp.dot(before.astype(BF16), to_owner.astype(BF16), preferred_element_type=F32)
    rank = jnp.sum(jnp.where(to_owner, count, 0.0), axis=1).astype(jnp.int32)
    return owner * owner_slots + rank


def lora(tokens, adapter_down, adapter_up, adapter_id, groups, tp):
    n, d = tokens.shape
    per_group, rank, _ = adapter_down.shape
    ho = adapter_up.shape[2]
    slots = groups * owner_slots
    slot = slot_of_request(adapter_id, groups, per_group)
    place = (lax.broadcasted_iota(jnp.int32, (slots, n), 0) == slot[None, :]).astype(BF16)
    out_rows = jnp.dot(place, tokens, preferred_element_type=F32).astype(BF16)
    local = (adapter_id % per_group).astype(BF16)
    out_ids = jnp.dot(place, local[:, None], preferred_element_type=F32).astype(BF16)
    out_ids = out_ids.reshape(groups, 1, owner_slots)
    out_ids = jnp.pad(out_ids, ((0, 0), (0, 7), (0, d - owner_slots)))
    sent = jnp.concatenate([out_rows.reshape(groups, owner_slots, d), out_ids], axis=1)
    here = lax.all_to_all(sent, "group", 0, 0, tiled=True)
    rows = here[:, :owner_slots].reshape(slots, d)
    ids = here[:, owner_slots, :owner_slots].astype(jnp.int32).reshape(1, 1, slots)
    mine = lax.broadcasted_iota(jnp.int32, (per_group, 1, slots), 0) == ids
    part = lax.dot_general(
        adapter_down.reshape(per_group * rank, d),
        rows,
        (((1,), (1,)), ((), ())),
        preferred_element_type=F32,
    ).reshape(per_group, rank, slots)
    part = jnp.sum(jnp.where(mine, part, 0.0), axis=0)
    share = rank // tp
    part = lax.all_to_all(part.astype(BF16).reshape(tp, share, slots), "tp", 0, 0, tiled=True)
    scaled = (adapter_scale_factor * jnp.sum(part.astype(F32), axis=0)).astype(BF16)
    scaled = lax.all_to_all(
        jnp.broadcast_to(scaled[None], (tp, share, slots)), "tp", 0, 0, tiled=True
    ).reshape(1, rank, slots)
    spread = jnp.where(mine, scaled, jnp.zeros((), BF16)).reshape(per_group * rank, slots)
    delta = lax.dot_general(
        spread,
        adapter_up.reshape(per_group * rank, ho),
        (((0,), (0,)), ((), ())),
        preferred_element_type=F32,
    ).astype(BF16)
    delta = lax.all_to_all(delta.reshape(groups, owner_slots, ho), "group", 0, 0, tiled=True)
    return lax.dot_general(
        place, delta.reshape(slots, ho), (((0,), (0,)), ((), ())), preferred_element_type=F32
    ).astype(BF16)


def solution(mesh):
    groups, tp = (mesh.shape["group"], mesh.shape["tp"])

    def on_device(tokens, w_query, adapter_down, adapter_up, adapter_id):
        gathered = lax.all_gather(tokens, "tp", axis=1, tiled=True)
        delta = lora(tokens, adapter_down, adapter_up, adapter_id, groups, tp)
        delta, gathered = lax.optimization_barrier((delta, gathered))
        base = lax.optimization_barrier(jnp.dot(gathered, w_query, preferred_element_type=F32))
        return (base + delta.astype(F32)).astype(BF16)

    placed = (
        P("group", "tp"),
        P(None, "tp"),
        P("group", None, "tp"),
        P("group", None, "tp"),
        P("group"),
    )
    return jax.shard_map(
        on_device, mesh=mesh, in_specs=placed, out_specs=P("group", "tp"), check_vma=False
    )
```

profile of v0, /device:TPU:1, one launch (start us, length us, event | category | flops | bytes accessed | tf_op | source)
XLA Modules:
  0.0 182.4 jit_solution(1290667721489595639)
XLA Ops:
  6.5 0.7 all-gather.2.cloned.1.call-update
  7.3 0.7 add_select_fusion.1
  8.0 0.4 fusion.13
  8.3 0.7 convert_add_fusion
  9.0 0.9 fusion.14
  9.9 0.1 reshape.91
  10.0 1.4 fusion.4
  11.4 0.1 fusion.10
  11.6 35.1 %all_to_all.20 = bf16[32,56,512]{2,1,0:T(8,128)(2,1)S(1)} all-to-all(bf16[32,56,512]{2,1,0:T(8,128)(2,1)S(1)} %fusion.10), channel_id=1, replica_groups=mesh['group'=32,'tp'=16] {'group'}, dimensions={0} | all-to-all | bytes 3670016 | tf_op jit(solution)/shard_map/all_to_all | solution.py:34
  46.8 0.2 slice.9
  47.0 0.7 fusion.24
  47.7 0.1 select_reduce_fusion
  47.9 0.5 broadcast.31
  48.4 0.7 reduce.7
  49.1 25.2 %all_to_all.21 = bf16[16,2,768]{2,1,0:T(2,128)(2,1)S(1)} all-to-all(bf16[16,2,768]{2,1,0:T(2,128)(2,1)S(1)} %reshape.99), channel_id=1, replica_groups=mesh['group'=32,'tp'=16] {'tp'}, dimensions={0} | all-to-all | bytes 98304 | tf_op jit(solution)/shard_map/all_to_all | solution.py:46
  74.3 0.1 convert_reduce_fusion
  74.5 0.9 reduce.8
  75.5 15.6 %all_to_all.22 = bf16[16,2,768]{2,1,0:T(2,128)(2,1)S(1)} all-to-all(bf16[16,2,768]{2,1,0:T(2,128)(2,1)S(1)} %reshape.101), channel_id=1, replica_groups=mesh['group'=32,'tp'=16] {'tp'}, dimensions={0} | all-to-all | bytes 98304 | tf_op jit(solution)/shard_map/all_to_all | solution.py:48
  91.2 0.4 fusion.5
  91.6 19.7 %all_to_all.23 = bf16[32,48,256]{2,1,0:T(8,128)(2,1)S(1)} all-to-all(bf16[32,48,256]{2,1,0:T(8,128)(2,1)S(1)} %bitcast.30), channel_id=1, replica_groups=mesh['group'=32,'tp'=16] {'group'}, dimensions={0} | all-to-all | bytes 1572864 | tf_op jit(solution)/shard_map/all_to_all | solution.py:58
  111.3 1.4 fusion.11
  112.7 54.4 %all-gather.2.cloned.1.call-done = bf16[768,8192]{1,0:T(8,128)(2,1)} async-done(((bf16[768,512]{1,0:T(8,128)(2,1)}), bf16[768,8192]{1,0:T(8,128)(2,1)}) %all-gather.2.cloned.1.call-update) | async-done | bytes 12582928 | tf_op jit(solution)/shard_map/all_gather | solution.py:68
  167.0 7.6 %fusion.25 = f32[768,256]{1,0:T(8,128)S(1)} fusion(bf16[768,8192]{1,0:T(8,128)(2,1)} %all-gather.2.cloned.1.call-done, bf16[8192,256]{1,0:T(8,128)(2,1)} %param.6), kind=kOutput, calls=%fused_computation.43 | convolution fusion | flops 3221225472 | bytes 17563648 | tf_op jit(solution)/shard_map/dot_general | solution.py:71
  174.7 0.9 add_convert_fusion
  (18 shorter events, 0.4 us)
Async XLA Ops:
  6.5 40.5 %copy-start = (bf16[12,16,512]{2,1,0:T(8,128)(2,1)S(1)}, bf16[12,16,512]{2,1,0:T(8,128)(2,1)}, u32[]{:S(2)}) copy-start(bf16[12,16,512]{2,1,0:T(8,128)(2,1)} %param.7) | copy-start | bytes 589828
  6.5 3.5 %copy-start.1 = (bf16[768,512]{1,0:T(8,128)(2,1)S(1)}, bf16[768,512]{1,0:T(8,128)(2,1)}, u32[]{:S(2)}) copy-start(bf16[768,512]{1,0:T(8,128)(2,1)} %param.5) | copy-start | bytes 2359300
  6.5 160.5 %all-gather.2.cloned.1.call-start = ((), (), s32[]{:S(2)}) async-start(), calls=%async_computation.4 | async-start | bytes 13369344 | tf_op jit(solution)/shard_map/all_gather | solution.py:68
  47.7 43.5 %copy-start.2 = (bf16[12,16,256]{2,1,0:T(8,128)(2,1)S(1)}, bf16[12,16,256]{2,1,0:T(8,128)(2,1)}, u32[]{:S(2)}) copy-start(bf16[12,16,256]{2,1,0:T(8,128)(2,1)} %param.8) | copy-start | bytes 294916
Sparse Core Ops, SparseCore 0:
  9.4 157.5 all-gather.1
where the time goes:
time: 183 us; the launch traced here: 182 us
  blocking collectives  95.6 us (52%)
  waiting for transfers between devices  55.1 us (30%)
  between operations  13.6 us (7%)
  matrix products  12.8 us (7%)
  other arithmetic  4.3 us (2%)
    all_gather x1, waiting for transfers between devices, on_device(): gathered = lax.all_gather(tokens, 'tp', axis=1, tiled=True)  54.4 us
    all_to_all x1, blocking collectives, lora(): here = lax.all_to_all(sent, 'group', 0, 0, tiled=True)  35.1 us
    all_to_all x1, blocking collectives, lora(): lax.all_to_all(part.astype(BF16).reshape(tp, share, slots), 'tp', 0, 0, t...  25.2 us
    all_to_all x1, blocking collectives, lora(): lax.all_to_all(delta.reshape(groups, owner_slots, ho), 'group', 0, 0, til...  19.7 us
    all_to_all x1, blocking collectives, lora(): lax.all_to_all(jnp.broadcast_to(scaled[None], (tp, share, slots)), 'tp',...  15.6 us
    dot_general x1, matrix products, on_device(): jnp.dot(gathered, w_query, preferred_element_type=F32)  7.62 us
  transfers between devices with their start and end apart: 1, of which 1 were waited for; matrix products, arithmetic and copies ran while one was open for 5% of the time, Pallas kernels for 0%

commit v1 on v0

--- a/solution.py
+++ b/solution.py
@@ -6,6 +6,11 @@
 adapter_scale_factor = 2.0
 owner_slots = 48
 F32, BF16 = (jnp.float32, jnp.bfloat16)
+
+
+def exchange_gather(block, axis, dim):
+    stack = jnp.stack([block] * lax.axis_size(axis))
+    return jnp.concatenate(lax.all_to_all(stack, axis, 0, 0), axis=dim)
 
 
 def slot_of_request(adapter_id, groups, per_group):
@@ -65,7 +70,7 @@
     groups, tp = (mesh.shape["group"], mesh.shape["tp"])
 
     def on_device(tokens, w_query, adapter_down, adapter_up, adapter_id):
-        gathered = lax.all_gather(tokens, "tp", axis=1, tiled=True)
+        gathered = exchange_gather(tokens, "tp", 1)
         delta = lora(tokens, adapter_down, adapter_up, adapter_id, groups, tp)
         delta, gathered = lax.optimization_barrier((delta, gathered))
         base = lax.optimization_barrier(jnp.dot(gathered, w_query, preferred_element_type=F32))

time: 183 us -> 667 us (3.64)
  waiting for transfers between devices: 55.1 us -> 555 us
  blocking collectives: 95.6 us -> 74.9 us
  between operations: 13.6 us -> 0.19 us
  starting transfers between devices: 0.01 us -> 10.6 us
    all_to_all x0 -> x2, waiting for transfers between devices: none -> 555 us  [the longest x1 541 us: exchange_gather(): return jnp.concatenate(lax.all_to_all(stack, axis, 0, 0), axis=dim)]
    all_gather x1 -> x0, waiting for transfers between devices: 54.4 us -> none  [on_device(): gathered = lax.all_gather(tokens, 'tp', axis=1, tiled=True)]
    all_to_all x1 -> x0, blocking collectives: 19.7 us -> none  [lora(): lax.all_to_all(delta.reshape(groups, owner_slots, ho), 'group', 0, 0, til...]
    all_to_all x0 -> x2, starting transfers between devices: none -> 10.6 us  [the longest x1 5.68 us: lora(): lax.all_to_all(delta.reshape(groups, owner_slots, ho), 'group', 0, 0, til...]
  transfers between devices with their start and end apart: 1 -> 2, of which waited for: 1 -> 2; matrix products, arithmetic and copies ran while one was open for 5% -> 0% of each run, Pallas kernels for 0% -> 0%
where the time goes in v1:
time: 667 us; the launch traced here: 666 us
  waiting for transfers between devices  555 us (83%)
  blocking collectives  74.9 us (11%)
  matrix products  13.7 us (2%)
  starting transfers between devices  10.6 us (2%)
  local copies, waits for them, and re-layouts  7.01 us (1%)
    all_to_all x1, waiting for transfers between devices, exchange_gather(): return jnp.concatenate(lax.all_to_all(stack, axis, 0, 0), axis=dim)  541 us
    all_to_all x1, blocking collectives, lora(): here = lax.all_to_all(sent, 'group', 0, 0, tiled=True)  35.1 us
    all_to_all x1, blocking collectives, lora(): lax.all_to_all(part.astype(BF16).reshape(tp, share, slots), 'tp', 0, 0, t...  25.1 us
    all_to_all x1, blocking collectives, lora(): lax.all_to_all(jnp.broadcast_to(scaled[None], (tp, share, slots)), 'tp',...  14.7 us
    all_to_all x1, waiting for transfers between devices, lora(): lax.all_to_all(delta.reshape(groups, owner_slots, ho), 'group', 0, 0, til...  14 us
  transfers between devices with their start and end apart: 2, of which 2 were waited for; matrix products, arithmetic and copies ran while one was open for 0% of the time, Pallas kernels for 0%

profile of v1, /device:TPU:1, one launch (start us, length us, event | category | flops | bytes accessed | tf_op | source)
XLA Modules:
  0.0 666.1 jit_solution(725666950054029827)
XLA Ops:
  0.0 0.8 add_select_fusion.1
  0.8 0.4 fusion.13
  1.1 0.7 convert_add_fusion
  1.9 0.9 fusion.14
  2.9 1.4 fusion.4
  4.3 0.1 fusion.10
  4.4 35.1 %all_to_all.25 = bf16[32,56,512]{2,1,0:T(8,128)(2,1)S(1)} all-to-all(bf16[32,56,512]{2,1,0:T(8,128)(2,1)S(1)} %fusion.10), channel_id=1, replica_groups=mesh['group'=32,'tp'=16] {'group'}, dimensions={0} | all-to-all | bytes 3670016 | tf_op jit(solution)/shard_map/all_to_all | solution.py:39
  39.7 0.2 slice.9
  39.9 0.7 fusion.24
  40.7 0.5 broadcast.33
  41.2 0.7 reduce.7
  41.9 25.1 %all_to_all.26 = bf16[16,2,768]{2,1,0:T(2,128)(2,1)S(1)} all-to-all(bf16[16,2,768]{2,1,0:T(2,128)(2,1)S(1)} %reshape.109), channel_id=1, replica_groups=mesh['group'=32,'tp'=16] {'tp'}, dimensions={0} | all-to-all | bytes 98304 | tf_op jit(solution)/shard_map/all_to_all | solution.py:51
  67.2 0.9 reduce.8
  68.1 14.7 %all_to_all.27 = bf16[16,2,768]{2,1,0:T(2,128)(2,1)S(1)} all-to-all(bf16[16,2,768]{2,1,0:T(2,128)(2,1)S(1)} %reshape.111), channel_id=1, replica_groups=mesh['group'=32,'tp'=16] {'tp'}, dimensions={0} | all-to-all | bytes 98304 | tf_op jit(solution)/shard_map/all_to_all | solution.py:53
  82.9 1.3 fusion.5
  84.2 5.7 all-to-all-start.3
  89.9 0.3 copy.12
  90.2 14.0 %all-to-all-done.3 = bf16[32,48,256]{2,1,0:T(8,128)(2,1)S(1)} async-done(((bf16[32,48,256]{2,1,0:T(8,128)(2,1)}), bf16[32,48,256]{2,1,0:T(8,128)(2,1)S(1)}, u32[]{:S(2)}, u32[]{:S(2)}) %all-to-all-start.3) | async-done | bytes 786464 | tf_op jit(solution)/shard_map/all_to_all | solution.py:63
  104.2 5.7 stack.2
  109.9 4.9 all-to-all-start.4
  114.9 1.4 fusion.11
  116.3 541.3 %all-to-all-done.4 = bf16[16,768,512]{1,2,0:T(8,128)(2,1)} async-done(((bf16[16,768,512]{1,2,0:T(8,128)(2,1)}), bf16[16,768,512]{1,2,0:T(8,128)(2,1)}, u32[]{:S(2)}, u32[]{:S(2)}) %all-to-all-start.4) | async-done | bytes 12582944 | tf_op jit(solution)/shard_map/all_to_all | solution.py:13
  657.6 7.7 %fusion.25 = f32[768,256]{1,0:T(8,128)S(1)} fusion(bf16[768,8192]{0,1:T(8,128)(2,1)} %bitcast.10, bf16[8192,256]{1,0:T(8,128)(2,1)} %param.6), kind=kOutput, calls=%fused_computation.43 | convolution fusion | flops 3221225472 | bytes 17563648 | tf_op jit(solution)/shard_map/dot_general | solution.py:76
  665.2 0.9 add_convert_fusion
  (20 shorter events, 0.7 us)
Async XLA Ops:
  0.0 39.9 %copy-start = (bf16[12,16,512]{2,1,0:T(8,128)(2,1)S(1)}, bf16[12,16,512]{2,1,0:T(8,128)(2,1)}, u32[]{:S(2)}) copy-start(bf16[12,16,512]{2,1,0:T(8,128)(2,1)} %param.7) | copy-start | bytes 589828
  0.0 2.9 copy-start.1
  40.5 42.4 %copy-start.2 = (bf16[12,16,256]{2,1,0:T(8,128)(2,1)S(1)}, bf16[12,16,256]{2,1,0:T(8,128)(2,1)}, u32[]{:S(2)}) copy-start(bf16[12,16,256]{2,1,0:T(8,128)(2,1)} %param.8) | copy-start | bytes 294916
  84.2 20.0 %all-to-all-start.3 = ((bf16[32,48,256]{2,1,0:T(8,128)(2,1)}), bf16[32,48,256]{2,1,0:T(8,128)(2,1)S(1)}, u32[]{:S(2)}, u32[]{:S(2)}) async-start(bf16[32,48,256]{2,1,0:T(8,128)(2,1)} %bitcast.7), calls=%async_computation.3 | async-start | bytes 1572864 | tf_op jit(solution)/shard_map/all_to_all | solution.py:63
  109.9 547.6 %all-to-all-start.4 = ((bf16[16,768,512]{1,2,0:T(8,128)(2,1)}), bf16[16,768,512]{1,2,0:T(8,128)(2,1)}, u32[]{:S(2)}, u32[]{:S(2)}) async-start(bf16[16,768,512]{1,2,0:T(8,128)(2,1)} %stack.2), calls=%async_computation.4 | async-start | bytes 25165824 | tf_op jit(solution)/shard_map/all_to_all | solution.py:13
